TPU v7x, 256 devices: a whole 4x4x8 slice. The times are simulated.
256 devices in a mesh: req: 16 (over y_hi, z), head: 16 (over y_lo, x, core).
Axes of the slice: x: 4, y: 4 (y_hi: 2, y_lo: 2; y = y_hi * 2 + y_lo), z: 8, core: 2. Of those that a mesh axis runs over, the one named last changes fastest.
Arguments:
- queries: bfloat16 [4096, 8192], P('req', 'head'), may hold values from -8 to 8
- new_keys: bfloat16 [4096, 1024], P('req'), may hold values from -5 to 5
- new_values: bfloat16 [4096, 1024], P('req'), may hold values from -24 to 24
- cache_keys: bfloat16 [32, 256, 1024], P('req'), may hold values from -4 to 4
- cache_values: bfloat16 [32, 256, 1024], P('req'), may hold values from -24 to 24
- request_slot: int32 [16], P('req'), may hold values from 0 to 1
- tenant_ids: int32 [4096], P('req'), may hold values from 0 to 255
- out_weight: bfloat16 [8192, 8192], P('req', 'head'), may hold values from -0.0625 to 0.0625
- adapter_down: bfloat16 [8192, 8192], P('head', 'req'), may hold values from -0.0625 to 0.0625
- adapter_up: bfloat16 [8192, 8192], P('req', 'head'), may hold values from -1 to 1
Outputs:
- mixed: bfloat16 [4096, 8192], P('req', 'head')
All inputs are finite; a program needn't handle non-finite values.
Results may differ from a plain program's by a relative error of at most 0.0064.
Values may be sent and summed in bfloat16 or wider, within the bound.
No kernel may reach another device: no remote copies, remote signals or barrier semaphores. Data moves between devices by JAX's collectives and lax.ppermute only.
A program may use at most 128 MiB of HBM per device.

v0:
```python
import jax
import jax.numpy as jnp
from jax import lax
from jax.sharding import PartitionSpec as P

HEADS = 64
HD = 128
KVH = 8
RANK = 32


def pick_heads(block, shared_index):
    spread = block.reshape(block.shape[0], KVH, HD)
    return jnp.take(spread, shared_index, axis=1)


def select(tenants, count):
    return tenants[:, None] == jnp.arange(count, dtype=jnp.int32)[None, :]


def shrink(block, tenants, weights):
    count = weights.shape[1] // RANK
    product = jnp.dot(block, weights, preferred_element_type=jnp.float32)
    product = product.reshape(block.shape[0], count, RANK)
    chosen = select(tenants, count).astype(jnp.float32)
    return jnp.sum(product * chosen[:, :, None], axis=1)


def expand(shrunk, tenants, weights):
    count = weights.shape[0] // RANK
    chosen = select(tenants, count).astype(jnp.bfloat16)
    spread = (chosen[:, :, None] * shrunk[:, None, :]).reshape(shrunk.shape[0], count * RANK)
    return jnp.dot(spread, weights, preferred_element_type=jnp.float32)


def attention(queries, new_keys, new_values, cache_keys, cache_values, request_slot):
    row_count = queries.shape[0]
    local_heads = queries.shape[1] // HD
    group = HEADS // KVH
    shared_index = (
        lax.axis_index("head") * local_heads + jnp.arange(local_heads, dtype=jnp.int32)
    ) // group
    slot_index = request_slot[0]
    keys_old = pick_heads(
        lax.dynamic_index_in_dim(cache_keys, slot_index, 0, keepdims=False), shared_index
    )
    values_old = pick_heads(
        lax.dynamic_index_in_dim(cache_values, slot_index, 0, keepdims=False), shared_index
    )
    keys_new = pick_heads(new_keys, shared_index)
    values_new = pick_heads(new_values, shared_index)
    split_queries = queries.reshape(row_count, local_heads, HD)
    scale = HD ** (-0.5)
    scores_old = (
        jnp.einsum("qhd,khd->hqk", split_queries, keys_old, preferred_element_type=jnp.float32)
        * scale
    )
    scores_new = (
        jnp.einsum("qhd,khd->hqk", split_queries, keys_new, preferred_element_type=jnp.float32)
        * scale
    )
    causal = (
        jnp.arange(row_count, dtype=jnp.int32)[:, None]
        >= jnp.arange(row_count, dtype=jnp.int32)[None, :]
    )
    scores_new = jnp.where(causal[None], scores_new, -1e30)
    highest = jnp.maximum(jnp.max(scores_old, axis=2), jnp.max(scores_new, axis=2))[:, :, None]
    weights_old = jnp.exp(scores_old - highest)
    weights_new = jnp.where(causal[None], jnp.exp(scores_new - highest), 0.0)
    total = jnp.sum(weights_old, axis=2, keepdims=True) + jnp.sum(
        weights_new, axis=2, keepdims=True
    )
    probs_old = (weights_old / total).astype(jnp.bfloat16)
    probs_new = (weights_new / total).astype(jnp.bfloat16)
    output = jnp.einsum("hqk,khd->qhd", probs_old, values_old, preferred_element_type=jnp.float32)
    output = output + jnp.einsum(
        "hqk,khd->qhd", probs_new, values_new, preferred_element_type=jnp.float32
    )
    return output.reshape(row_count, local_heads * HD).astype(jnp.bfloat16)


def local(
    queries,
    new_keys,
    new_values,
    cache_keys,
    cache_values,
    request_slot,
    tenant_ids,
    out_weight,
    adapter_down,
    adapter_up,
):
    attended = attention(queries, new_keys, new_values, cache_keys, cache_values, request_slot)
    partial_value = shrink(
        attended, tenant_ids, lax.all_gather(adapter_down, "req", axis=1, tiled=True)
    )
    shrunk = lax.psum(partial_value, "head").astype(jnp.bfloat16)
    columns = lax.all_gather(out_weight, "req", axis=0, tiled=True)
    rows_block = lax.all_to_all(columns, "head", split_axis=0, concat_axis=1, tiled=True)
    base_term = jnp.dot(attended, rows_block, preferred_element_type=jnp.float32)
    base = lax.psum_scatter(base_term, "head", scatter_dimension=1, tiled=True)
    summed = expand(shrunk, tenant_ids, lax.all_gather(adapter_up, "req", axis=0, tiled=True))
    delta = lax.optimization_barrier(summed.astype(jnp.bfloat16)).astype(jnp.float32)
    return (base + delta).astype(jnp.bfloat16)


def solution(mesh):
    placed = (
        P("req", "head"),
        P("req", None),
        P("req", None),
        P("req", None, None),
        P("req", None, None),
        P("req"),
        P("req"),
        P("req", "head"),
        P("head", "req"),
        P("req", "head"),
    )
    return jax.shard_map(
        local, mesh=mesh, in_specs=placed, out_specs=P("req", "head"), check_vma=False
    )
```

profile of v0, /device:TPU:16, one launch (start us, length us, event | category | flops | bytes accessed | tf_op | source)
XLA Modules:
  0.0 553.8 jit_solution(7732991442768242154)
XLA Ops:
  6.5 0.7 all-gather.4.cloned.1.call-update
  7.3 2.1 copy.41
  9.5 0.7 all-gather.8.cloned.1.call-update
  10.1 135.3 %all-gather.4.cloned.1.call-done = bf16[8192,512]{1,0:T(8,128)(2,1)} async-done(((bf16[512,512]{1,0:T(8,128)(2,1)}), bf16[8192,512]{1,0:T(8,128)(2,1)}) %all-gather.4.cloned.1.call-update) | async-done | bytes 8388624 | tf_op jit(solution)/shard_map/all_gather | solution.py:99
  145.4 6.1 %all-to-all-start = ((bf16[16,512,512]{2,1,0:T(8,128)(2,1)}), bf16[16,512,512]{2,1,0:T(8,128)(2,1)}, u32[]{:S(2)}, u32[]{:S(2)}) async-start(bf16[16,512,512]{2,1,0:T(8,128)(2,1)} %bitcast.65), calls=%async_computation | async-start | bytes 16777216 | tf_op jit(solution)/shard_map/all_to_all | solution.py:100
  152.3 1.1 constant_dynamic-slice_fusion
  154.4 0.6 gather_fusion.1
  155.0 0.6 gather_fusion.2
  156.1 0.6 gather_fusion
  157.2 0.6 gather_fusion.3
  159.0 0.4 fusion.13
  159.4 0.5 fusion.7
  159.9 104.5 %all-to-all-done = bf16[16,512,512]{2,1,0:T(8,128)(2,1)} async-done(((bf16[16,512,512]{2,1,0:T(8,128)(2,1)}), bf16[16,512,512]{2,1,0:T(8,128)(2,1)}, u32[]{:S(2)}, u32[]{:S(2)}) %all-to-all-start) | async-done | bytes 8388640 | tf_op jit(solution)/shard_map/all_to_all | solution.py:100
  264.4 12.3 %copy.40 = bf16[512,16,512]{0,2,1:T(8,128)(2,1)} copy(bf16[512,16,512]{2,0,1:T(8,128)(2,1)} %bitcast.14) | data formatting | bytes 16777216 | tf_op jit(solution)/shard_map/all_to_all | solution.py:100
  276.8 9.0 %fusion.44 = f32[256,8192]{1,0:T(8,128)} fusion(bf16[256,512]{0,1:T(8,128)(2,1)S(1)} %bitcast.70, bf16[512,8192]{0,1:T(8,128)(2,1)} %bitcast.63), kind=kOutput, calls=%fused_computation.68 | convolution fusion | flops 2147483648 | bytes 17039360 | tf_op jit(solution)/shard_map/dot_general | solution.py:101
  285.8 0.7 copy-done.5
  286.5 40.1 %all-gather.6.cloned.1.call-done = bf16[512,8192]{0,1:T(8,128)(2,1)} async-done(((bf16[512,512]{0,1:T(8,128)(2,1)}), bf16[512,8192]{0,1:T(8,128)(2,1)}) %all-gather.6.cloned.1.call-update) | async-done | bytes 8388624 | tf_op jit(solution)/shard_map/all_gather | solution.py:96
  326.6 12.9 %multiply_reduce_fusion = f32[256,32]{0,1:T(8,128)S(1)} fusion(f32[256,256]{0,1:T(8,128)S(1)} %get-tuple-element.9, bf16[256,512,1]{0,1,2:T(8,128)(2,1)S(1)} %bitcast.71, bf16[256,32,512]{2,1,0:T(8,128)(2,1)} %bitcast.72), kind=kOutput, calls=%fused_computation.6 | convolution fusion | flops 2151669760 | bytes 8945664 | tf_op jit(solution)/shard_map/dot_general | solution.py:23
  339.5 58.6 %psum.7 = bf16[256,32]{0,1:T(8,128)(2,1)S(1)} all-reduce(f32[256,32]{0,1:T(8,128)S(1)} %multiply_reduce_fusion), channel_id=1, replica_groups=mesh['req'=16,'head'=16] {'head'}, use_global_device_ids=true, to_apply=%region_6.8 | all-reduce | flops 8192 | bytes 49152 | tf_op jit(solution)/shard_map/psum | solution.py:98
  398.1 2.2 broadcast_multiply_fusion
  400.3 66.4 %all-gather.8.cloned.1.call-done = bf16[8192,512]{1,0:T(8,128)(2,1)} async-done(((bf16[512,512]{1,0:T(8,128)(2,1)}), bf16[8192,512]{1,0:T(8,128)(2,1)}) %all-gather.8.cloned.1.call-update) | async-done | bytes 8388624 | tf_op jit(solution)/shard_map/all_gather | solution.py:103
  466.8 7.0 %convolution_convert_fusion = bf16[256,512]{1,0:T(8,128)(2,1)S(1)} fusion(bf16[256,8192]{0,1:T(8,128)(2,1)} %bitcast.64, bf16[8192,512]{1,0:T(8,128)(2,1)} %all-gather.8.cloned.1.call-done), kind=kOutput, calls=%fused_computation.15 | convolution fusion | flops 2147614720 | bytes 12845056 | tf_op jit(solution)/shard_map/dot_general | solution.py:33
  473.8 71.6 %reduce-scatter.2.cloned.1.call-done = f32[256,512]{1,0:T(8,128)} async-done(((f32[256,8192]{1,0:T(8,128)}), f32[256,512]{1,0:T(8,128)}) %reduce-scatter.2.cloned.1.call-update) | async-done | bytes 524304 | tf_op jit(solution)/shard_map/reduce_scatter | solution.py:102
  545.4 1.8 add_convert_fusion
  (35 shorter events, 3.3 us)
Async XLA Ops:
  6.5 151.3 %copy-start = (bf16[256,512]{1,0:T(8,128)(2,1)S(1)}, bf16[256,512]{1,0:T(8,128)(2,1)}, u32[]{:S(2)}) copy-start(bf16[256,512]{1,0:T(8,128)(2,1)} %param.12) | copy-start | bytes 786436
  6.5 138.9 %all-gather.4.cloned.1.call-start = ((), (), s32[]{:S(2)}) async-start(), calls=%async_computation.2 | async-start | bytes 8912896 | tf_op jit(solution)/shard_map/all_gather | solution.py:99
  7.3 319.3 %all-gather.6.cloned.1.call-start = ((), (), s32[]{:S(2)}) async-start(), calls=%async_computation.4 | async-start | bytes 8912896 | tf_op jit(solution)/shard_map/all_gather | solution.py:96
  9.4 457.3 %all-gather.8.cloned.1.call-start = ((), (), s32[]{:S(2)}) async-start(), calls=%async_computation.5 | async-start | bytes 8912896 | tf_op jit(solution)/shard_map/all_gather | solution.py:103
  145.4 6.8 %copy-start.4 = (bf16[2,256,1024]{2,1,0:T(8,128)(2,1)S(1)}, bf16[2,256,1024]{2,1,0:T(8,128)(2,1)}, u32[]{:S(2)}) copy-start(bf16[2,256,1024]{2,1,0:T(8,128)(2,1)} %param.15) | copy-start | bytes 3145732
  145.4 8.5 %copy-start.2 = (bf16[256,1024]{1,0:T(8,128)(2,1)S(1)}, bf16[256,1024]{1,0:T(8,128)(2,1)}, u32[]{:S(2)}) copy-start(bf16[256,1024]{1,0:T(8,128)(2,1)} %param.13) | copy-start | bytes 1572868
  145.4 119.0 %all-to-all-start = ((bf16[16,512,512]{2,1,0:T(8,128)(2,1)}), bf16[16,512,512]{2,1,0:T(8,128)(2,1)}, u32[]{:S(2)}, u32[]{:S(2)}) async-start(bf16[16,512,512]{2,1,0:T(8,128)(2,1)} %bitcast.65), calls=%async_computation | async-start | bytes 16777216 | tf_op jit(solution)/shard_map/all_to_all | solution.py:100
  151.5 5.2 copy-start.3
  151.5 393.9 %reduce-scatter.2.cloned.1.call-start = ((), (), s32[]{:S(2)}) async-start(), calls=%async_computation.3 | async-start | bytes 8912896 | tf_op jit(solution)/shard_map/reduce_scatter | solution.py:102
  285.8 0.7 copy-start.5
  466.7 80.5 %copy-start.1 = (bf16[256,512]{1,0:T(8,128)(2,1)S(1)}, bf16[256,512]{1,0:T(8,128)(2,1)}, u32[]{:S(2)}) copy-start(bf16[256,512]{1,0:T(8,128)(2,1)} %param.12) | copy-start | bytes 786436
Sparse Core Ops, SparseCore 0:
  9.9 135.4 all-gather.3
  148.0 178.5 all-gather.5
  329.2 137.5 all-gather.7
  469.2 76.2 reduce-scatter.1
where the time goes:
time: 554 us
  waiting for transfers between devices  419 us (76%)
  blocking collectives  58.6 us (11%)
  matrix products  30.6 us (6%)
  local copies, waits for them, and re-layouts  20.5 us (4%)
  between operations  14 us (3%)
  starting transfers between devices  6.19 us (1%)
    all_gather x1, waiting for transfers between devices, local(): columns = lax.all_gather(out_weight, 'req', axis=0, tiled=True)  135 us
    all_to_all x1, waiting for transfers between devices, local(): lax.all_to_all(columns, 'head', split_axis=0, concat_axis=1, tiled=True)  105 us
    reduce_scatter x1, waiting for transfers between devices, local(): base = lax.psum_scatter(base_term, 'head', scatter_dimension=1, tiled=True)  71.6 us
    all_gather x1, waiting for transfers between devices, local(): lax.all_gather(adapter_up, 'req', axis=0, tiled=True)  66.4 us
    psum x1, blocking collectives, local(): shrunk = lax.psum(partial_value, 'head').astype(jnp.bfloat16)  58.6 us
    all_gather x1, waiting for transfers between devices, local(): lax.all_gather(adapter_down, 'req', axis=1, tiled=True)  40.1 us
    dot_general x1, matrix products, shrink(): product = jnp.dot(block, weights, preferred_element_type=jnp.float32)  12.9 us
    all_to_all x1, local copies, waits for them, and re-layouts, local(): lax.all_to_all(columns, 'head', split_axis=0, concat_axis=1, tiled=True)  12.3 us
  transfers between devices with their start and end apart: 5, of which 5 were waited for; matrix products, arithmetic and copies ran while one was open for 10% of the time, Pallas kernels for 0%

commit v1 on v0

v1 whole, which is shorter than its diff:
```python
import jax
import jax.numpy as jnp
from jax import lax
from jax.experimental import pallas as pl
from jax.experimental.pallas import tpu as pltpu
from jax.sharding import Mesh
from jax.sharding import PartitionSpec as P

HD = 128
RANK = 32
ROWS = 256
BF = jnp.bfloat16
F32 = jnp.float32
AXES = ("yh", "z", "yl", "x", "c")
REQ = ("yh", "z")
HEAD = ("yl", "x", "c")


def dot_nt(a, b):
    return lax.dot_general(a, b, (((1,), (1,)), ((), ())), preferred_element_type=F32)


def dot(a, b):
    return jnp.dot(a, b, preferred_element_type=F32)


def attend_kernel(where_ref, q_ref, ko_ref, vo_ref, kn_ref, vn_ref, out_ref):
    scale = HD**-0.5
    keys_old, values_old = ko_ref[0], vo_ref[0]
    keys_new, values_new = kn_ref[...], vn_ref[...]
    rows = q_ref.shape[0]
    causal = lax.broadcasted_iota(jnp.int32, (rows, rows), 0) >= lax.broadcasted_iota(
        jnp.int32, (rows, rows), 1
    )
    for head in range(q_ref.shape[1] // HD):
        cols = slice(head * HD, (head + 1) * HD)
        query = q_ref[:, cols]
        scores_old = dot_nt(query, keys_old) * scale
        scores_new = jnp.where(causal, dot_nt(query, keys_new) * scale, -1e30)
        highest = jnp.maximum(
            jnp.max(scores_old, axis=1, keepdims=True), jnp.max(scores_new, axis=1, keepdims=True)
        )
        weights_old = jnp.exp(scores_old - highest)
        weights_new = jnp.where(causal, jnp.exp(scores_new - highest), 0.0)
        total = jnp.sum(weights_old, axis=1, keepdims=True) + jnp.sum(
            weights_new, axis=1, keepdims=True
        )
        inverse = 1.0 / total
        probs_old = (weights_old * inverse).astype(BF)
        probs_new = (weights_new * inverse).astype(BF)
        out_ref[:, cols] = (dot(probs_old, values_old) + dot(probs_new, values_new)).astype(BF)


def attend(queries, new_keys, new_values, cache_keys, cache_values, where):
    rows, width = queries.shape
    keys = cache_keys.shape[1]
    return pl.pallas_call(
        attend_kernel,
        out_shape=jax.ShapeDtypeStruct((rows, width), BF),
        grid_spec=pltpu.PrefetchScalarGridSpec(
            num_scalar_prefetch=1,
            grid=(1,),
            in_specs=[
                pl.BlockSpec((rows, width), lambda i, w: (0, 0)),
                pl.BlockSpec((1, keys, HD), lambda i, w: (w[0], 0, w[1])),
                pl.BlockSpec((1, keys, HD), lambda i, w: (w[0], 0, w[1])),
                pl.BlockSpec((rows, HD), lambda i, w: (0, w[1])),
                pl.BlockSpec((rows, HD), lambda i, w: (0, w[1])),
            ],
            out_specs=pl.BlockSpec((rows, width), lambda i, w: (0, 0)),
        ),
        name="attend",
    )(where, queries, cache_keys, cache_values, new_keys, new_values)


def fold(value):
    value = value + pltpu.roll(value, 64, 1)
    return value + pltpu.roll(value, 32, 1)


def lane_group(shape):
    return lax.broadcasted_iota(jnp.int32, shape, 1) // RANK


def shrink_kernel(base_ref, att_ref, down_a_ref, down_b_ref, ids_ref, out_ref):
    step = pl.program_id(0)
    ids = ids_ref[...].astype(F32).astype(jnp.int32)
    group = lane_group(ids.shape)
    total = jnp.zeros(ids.shape, F32)
    for which, down_ref in enumerate((down_a_ref, down_b_ref)):
        product = dot(att_ref[...], down_ref[...])
        local = ids - base_ref[which]
        for part in range(product.shape[1] // 128):
            hit = local == group + part * 4
            total = total + jnp.where(hit, product[:, part * 128 : (part + 1) * 128], 0.0)
    total = jnp.where(group == step // 2, fold(total), 0.0)
    half = pl.ds(pl.multiple_of((step % 2) * ROWS, ROWS), ROWS)

    @pl.when(step < 2)
    def _():
        out_ref[half, :] = total

    @pl.when(step >= 2)
    def _():
        out_ref[half, :] += total


def shrink(attended, down_a, down_b, ids, bases):
    depth, width = down_a.shape
    return pl.pallas_call(
        shrink_kernel,
        out_shape=jax.ShapeDtypeStruct((2 * ROWS, 128), F32),
        grid_spec=pltpu.PrefetchScalarGridSpec(
            num_scalar_prefetch=1,
            grid=(8,),
            in_specs=[
                pl.BlockSpec((ROWS, depth), lambda i, w: (i, 0)),
                pl.BlockSpec((depth, width), lambda i, w: (0, 0)),
                pl.BlockSpec((depth, width), lambda i, w: (0, 0)),
                pl.BlockSpec((ROWS, 128), lambda i, w: (i, 0)),
            ],
            out_specs=pl.BlockSpec((2 * ROWS, 128), lambda i, w: (0, 0)),
        ),
        name="shrink",
    )(bases, attended, down_a, down_b, ids)


def project_kernel(
    base_ref, att_a_ref, att_b_ref, w_a_ref, w_b_ref, up_a_ref, up_b_ref, small_ref, ids_ref, out_ref
):
    step = pl.program_id(0)
    ids = ids_ref[...].astype(F32).astype(jnp.int32)
    group = lane_group(ids.shape)
    half = pl.ds(pl.multiple_of((step % 2) * ROWS, ROWS), ROWS)
    small = small_ref[half, :].astype(F32)
    small = fold(jnp.where(group == step // 2, small, 0.0))
    delta = jnp.zeros(out_ref.shape, F32)
    for which, up_ref in enumerate((up_a_ref, up_b_ref)):
        local = ids - base_ref[which]
        spread = [
            jnp.where(local == group + part * 4, small, 0.0).astype(BF)
            for part in range(up_ref.shape[0] // 128)
        ]
        delta = delta + dot(jnp.concatenate(spread, axis=1), up_ref[...])
    base = dot(att_a_ref[0], w_a_ref[...]) + dot(att_b_ref[0], w_b_ref[...])
    out_ref[...] = base + delta.astype(BF).astype(F32)


def project(gathered, w_a, w_b, up_a, up_b, small, ids, bases):
    depth, width = w_a.shape
    whole = pl.BlockSpec((depth, width), lambda i, w: (0, 0))
    return pl.pallas_call(
        project_kernel,
        out_shape=jax.ShapeDtypeStruct((8 * ROWS, width), F32),
        grid_spec=pltpu.PrefetchScalarGridSpec(
            num_scalar_prefetch=1,
            grid=(8,),
            in_specs=[
                pl.BlockSpec((1, ROWS, depth), lambda i, w: (w[2] * 8 + i, 0, 0)),
                pl.BlockSpec((1, ROWS, depth), lambda i, w: ((1 - w[2]) * 8 + i, 0, 0)),
                whole,
                whole,
                whole,
                whole,
                pl.BlockSpec((2 * ROWS, 128), lambda i, w: (0, 0)),
                pl.BlockSpec((ROWS, 128), lambda i, w: (i, 0)),
            ],
            out_specs=pl.BlockSpec((ROWS, width), lambda i, w: (i, 0)),
        ),
        name="project",
    )(bases, gathered, gathered, w_a, w_b, up_a, up_b, small, ids)


SWAP = [(0, 1), (1, 0)]
TURN = [
    (z * 8 + x * 2 + c, (x * 2 + c) * 8 + z) for z in range(8) for x in range(4) for c in range(2)
]


def local(
    queries,
    new_keys,
    new_values,
    cache_keys,
    cache_values,
    request_slot,
    tenant_ids,
    out_weight,
    adapter_down,
    adapter_up,
):
    yh, z = lax.axis_index("yh"), lax.axis_index("z")
    head = lax.axis_index(HEAD)
    tenants = adapter_up.shape[0] // RANK
    bases = jnp.stack([(yh * 8 + z) * tenants, ((1 - yh) * 8 + z) * tenants, yh]).astype(jnp.int32)
    where = jnp.stack([request_slot[0], head // 2]).astype(jnp.int32)

    down_b = lax.ppermute(adapter_down, "yh", SWAP)
    w_b = lax.ppermute(out_weight, "yh", SWAP)
    up_b = lax.ppermute(adapter_up, "yh", SWAP)
    ids = jnp.broadcast_to(tenant_ids[:, None], (ROWS, 128)).astype(BF)
    ids = lax.all_gather(lax.optimization_barrier(ids), "z", axis=0, tiled=True)

    attended = attend(queries, new_keys, new_values, cache_keys, cache_values, where)
    in_place = lax.all_gather(attended, "z", axis=0, tiled=True)
    turned = lax.ppermute(attended, ("z", "x", "c"), TURN)
    gathered = lax.all_gather(turned, HEAD, axis=0, tiled=False)

    packed = shrink(in_place, adapter_down, down_b, ids, bases)
    pieces = lax.all_to_all(packed.reshape(16, 32, 128), HEAD, 0, 0, tiled=False)
    small = jnp.sum(pieces, axis=0).astype(BF)
    small = lax.all_gather(small, HEAD, axis=0, tiled=True)

    partial_sum = project(gathered, out_weight, w_b, adapter_up, up_b, small, ids, bases)
    mixed = lax.psum_scatter(partial_sum, "z", scatter_dimension=0, tiled=True)
    return mixed.astype(BF)


def solution(mesh):
    fine = Mesh(mesh.devices.reshape(2, 8, 2, 4, 2), AXES)
    placed = (
        P(REQ, HEAD),
        P(REQ, None),
        P(REQ, None),
        P(REQ, None, None),
        P(REQ, None, None),
        P(REQ),
        P(REQ),
        P(REQ, HEAD),
        P(HEAD, REQ),
        P(REQ, HEAD),
    )
    return jax.shard_map(
        local, mesh=fine, in_specs=placed, out_specs=P(REQ, HEAD), check_vma=False
    )
```

time: 554 us -> 197 us (0.36)
  waiting for transfers between devices: 419 us -> 52 us
  blocking collectives: 58.6 us -> 92.5 us
  matrix products: 30.6 us -> 0 us
  Pallas kernels: 0 us -> 24.4 us
  local copies, waits for them, and re-layouts: 20.5 us -> 2.53 us
    all_gather x3 -> x2, waiting for transfers between devices: 242 us -> 0.04 us  [the longest x1 0.02 us: local(): gathered = lax.all_gather(turned, HEAD, axis=0, tiled=False)]
    all_to_all x1 -> x0, waiting for transfers between devices: 105 us -> none  [local(): lax.all_to_all(columns, 'head', split_axis=0, concat_axis=1, tiled=True)]
    all_gather x0 -> x2, blocking collectives: none -> 79.7 us  [the longest x1 59.2 us: local(): ids = lax.all_gather(lax.optimization_barrier(ids), 'z', axis=0, tiled=True)]
    psum x1 -> x0, blocking collectives: 58.6 us -> none  [local(): shrunk = lax.psum(partial_value, 'head').astype(jnp.bfloat16)]
    dot_general x7 -> x0, matrix products: 30.6 us -> none  [the longest x1 12.9 us: shrink(): product = jnp.dot(block, weights, preferred_element_type=jnp.float32)]
    pallas_call x0 -> x3, Pallas kernels: none -> 24.4 us  [the longest x1 11.6 us: project(): pl.pallas_call(project_kernel, out_shape=jax.ShapeDtypeStruct((8 * ROWS,...]
    reduce_scatter x1, waiting for transfers between devices: 71.6 us -> 51.9 us  [local(): mixed = lax.psum_scatter(partial_sum, 'z', scatter_dimension=0, tiled=True)]
    all_to_all x0 -> x1, blocking collectives: none -> 12.7 us  [local(): lax.all_to_all(packed.reshape(16, 32, 128), HEAD, 0, 0, tiled=False)]
  transfers between devices with their start and end apart: 5 -> 7, of which waited for: 5 -> 1; matrix products, arithmetic and copies ran while one was open for 10% -> 0% of each run, Pallas kernels for 0% -> 4%
where the time goes in v1:
time: 197 us; the launch traced here: 196 us
  blocking collectives  92.5 us (47%)
  waiting for transfers between devices  52 us (26%)
  Pallas kernels  24.4 us (12%)
  between operations  13.9 us (7%)
  starting transfers between devices  7.39 us (4%)
  other arithmetic  3.12 us (2%)
  local copies, waits for them, and re-layouts  2.53 us (1%)
    all_gather x1, blocking collectives, local(): ids = lax.all_gather(lax.optimization_barrier(ids), 'z', axis=0, tiled=True)  59.2 us
    reduce_scatter x1, waiting for transfers between devices, local(): mixed = lax.psum_scatter(partial_sum, 'z', scatter_dimension=0, tiled=True)  51.9 us
    all_gather x1, blocking collectives, local(): small = lax.all_gather(small, HEAD, axis=0, tiled=True)  20.5 us
    all_to_all x1, blocking collectives, local(): lax.all_to_all(packed.reshape(16, 32, 128), HEAD, 0, 0, tiled=False)  12.7 us
    pallas_call x1, Pallas kernels, project(): pl.pallas_call(project_kernel, out_shape=jax.ShapeDtypeStruct((8 * ROWS,...  11.6 us
    pallas_call x1, Pallas kernels, shrink(): pl.pallas_call(shrink_kernel, out_shape=jax.ShapeDtypeStruct((2 * ROWS, 1...  8.67 us
    pallas_call x1, Pallas kernels, attend(): pl.pallas_call(attend_kernel, out_shape=jax.ShapeDtypeStruct((rows, width...  4.14 us
  transfers between devices with their start and end apart: 7, of which 1 were waited for; matrix products, arithmetic and copies ran while one was open for 0% of the time, Pallas kernels for 4%

profile of v1, /device:TPU:16, one launch (start us, length us, event | category | flops | bytes accessed | tf_op | source)
XLA Modules:
  0.0 195.9 jit_solution(3768688487936754403)
XLA Ops:
  6.5 0.0 all-gather.4.cloned.1.call-start
  7.4 0.6 pad_add_fusion.1.where_ref
  8.0 4.1 %attend.1 = bf16[256,512]{1,0:T(8,128)(2,1)} custom-call(s32[2]{0:T(128)} %pad_add_fusion.1.where_ref, bf16[256,512]{1,0:T(8,128)(2,1)} %q_ref.1, bf16[2,256,1024]{2,1,0:T(8,128)(2,1)} %ko_ref.1, bf16[2,256,1024]{2,1,0:T(8,128)(2,1)} %vo_ref.1, bf16[256,1024]{1,0:T(8,128)(2,1)} %kn_ref.1, bf16[256,1024]{1,0:T(8,128)(2,1)} %vn_ref.1), custom_call_target="tpu_custom_call" | custom-call | tf_op jit(solution)/shard_map/attend/pallas_call | solution.py:57
  12.1 0.0 all-gather.4.cloned.1.call-update
  12.2 0.0 all-gather.6.cloned.1.call-start
  12.2 1.6 collective-permute-start
  13.8 0.7 copy-done.6
  14.6 0.0 reduce-scatter.2.cloned.1.call-start
  14.6 2.1 %collective-permute-start.3 = (bf16[512,512]{1,0:T(8,128)(2,1)S(1)}, bf16[512,512]{1,0:T(8,128)(2,1)S(1)}, u32[]{:S(2)}, u32[]{:S(2)}) collective-permute-start(bf16[512,512]{1,0:T(8,128)(2,1)S(1)} %copy-done), channel_id=1, source_target_pairs={{0,128},{128,0},{1,129},{129,1},{2,130},{130,2},{3,131},{131,3},{4... | collective-permute-start | bytes 1572872 | tf_op jit(solution)/shard_map/ppermute | solution.py:198
  16.8 1.5 collective-permute-start.1
  18.2 2.0 %collective-permute-start.2 = (bf16[512,512]{1,0:T(8,128)(2,1)S(1)}, bf16[512,512]{1,0:T(8,128)(2,1)S(1)}, u32[]{:S(2)}, u32[]{:S(2)}) collective-permute-start(bf16[512,512]{1,0:T(8,128)(2,1)S(1)} %copy-done.2), channel_id=1, source_target_pairs={{0,128},{128,0},{1,129},{129,1},{2,130},{130,2},{3,131},{131,3},{4... | collective-permute-start | bytes 1572872 | tf_op jit(solution)/shard_map/ppermute | solution.py:200
  20.3 0.1 broadcast_in_dim.2
  20.4 0.7 pad_add_fusion.base_ref
  21.1 59.2 %all_gather.18.ids_ref = bf16[2048,128]{1,0:T(8,128)(2,1)} all-gather(bf16[256,128]{1,0:T(8,128)(2,1)S(1)} %broadcast_in_dim.2), channel_id=1, replica_groups=mesh['yh'=2,'z'=8,'yl'=2,'x'=4,'c'=2] {'z'}, dimensions={0}, use_global_device_ids=true | all-gather | bytes 589824 | tf_op jit(solution)/shard_map/all_gather | solution.py:202
  80.3 0.8 copy-done.5
  81.1 8.7 %shrink.1 = f32[512,128]{1,0:T(8,128)} custom-call(s32[3]{0:T(128)} %pad_add_fusion.base_ref, bf16[2048,512]{1,0:T(8,128)(2,1)} %all-gather.4.cloned.1.call-done.att_ref, bf16[512,512]{1,0:T(8,128)(2,1)} %down_a_ref.1, bf16[512,512]{1,0:T(8,128)(2,1)} %copy-done.5, bf16[2048,128]{1,0:T(8,128)(2,1)} %all_gather.18.ids_ref), custom_call_target="tpu_custom_call" | custom-call | tf_op jit(solution)/shard_map/shrink/pallas_call | solution.py:110
  89.8 12.7 %all_to_all.5 = f32[16,32,128]{2,1,0:T(8,128)S(1)} all-to-all(f32[16,32,128]{2,1,0:T(8,128)} %bitcast.8), channel_id=1, replica_groups=mesh['yh'=2,'z'=8,'yl'=2,'x'=4,'c'=2] {'yl','x','c'}, dimensions={0} | all-to-all | bytes 524288 | tf_op jit(solution)/shard_map/all_to_all | solution.py:210
  102.5 20.5 %all_gather.19.small_ref = bf16[512,128]{1,0:T(8,128)(2,1)} all-gather(bf16[32,128]{1,0:T(8,128)(2,1)S(1)} %reduce_sum.9), channel_id=1, replica_groups=mesh['yh'=2,'z'=8,'yl'=2,'x'=4,'c'=2] {'yl','x','c'}, dimensions={0}, use_global_device_ids=true | all-gather | bytes 139264 | tf_op jit(solution)/shard_map/all_gather | solution.py:212
  123.1 0.0 all-gather.6.cloned.1.call-done
  123.1 0.8 copy-done.3
  123.9 0.1 copy-done.4
  124.0 11.6 %project.1 = f32[2048,512]{1,0:T(8,128)} custom-call(s32[3]{0:T(128)} %pad_add_fusion.base_ref, bf16[16,256,512]{2,1,0:T(8,128)(2,1)} %bitcast.6, bf16[16,256,512]{2,1,0:T(8,128)(2,1)} %bitcast.7, bf16[512,512]{1,0:T(8,128)(2,1)} %w_a_ref.1, bf16[512,512]{1,0:T(8,128)(2,1)} %copy-done.3, bf16[512,512]{1,0:T(8,128)(2,1)} %up_a_ref.1, ...), custom_call_target="tpu_custom_call" | custom-call | tf_op jit(solution)/shard_map/project/pallas_call | solution.py:152
  135.7 51.9 %reduce-scatter.2.cloned.1.call-done = f32[256,512]{1,0:T(8,128)} async-done(((f32[2048,512]{1,0:T(8,128)}), f32[256,512]{1,0:T(8,128)}) %reduce-scatter.2.cloned.1.call-update) | async-done | bytes 524304 | tf_op jit(solution)/shard_map/reduce_scatter | solution.py:215
  187.6 1.8 convert_element_type.12
  (21 shorter events, 0.1 us)
Async XLA Ops:
  6.5 8.1 %copy-start = (bf16[512,512]{1,0:T(8,128)(2,1)S(1)}, bf16[512,512]{1,0:T(8,128)(2,1)}, u32[]{:S(2)}) copy-start(bf16[512,512]{1,0:T(8,128)(2,1)} %down_a_ref.1) | copy-start | bytes 1572868
  6.5 10.2 %copy-start.1 = (bf16[512,512]{1,0:T(8,128)(2,1)S(1)}, bf16[512,512]{1,0:T(8,128)(2,1)}, u32[]{:S(2)}) copy-start(bf16[512,512]{1,0:T(8,128)(2,1)} %w_a_ref.1) | copy-start | bytes 1572868
  6.5 11.7 %copy-start.2 = (bf16[512,512]{1,0:T(8,128)(2,1)S(1)}, bf16[512,512]{1,0:T(8,128)(2,1)}, u32[]{:S(2)}) copy-start(bf16[512,512]{1,0:T(8,128)(2,1)} %up_a_ref.1) | copy-start | bytes 1572868
  6.5 13.8 %copy-start.7 = (s32[256]{0:T(256)S(1)}, s32[256]{0:T(256)}, u32[]{:S(2)}) copy-start(s32[256]{0:T(256)} %param.16) | copy-start | bytes 3076
  6.5 73.8 %all-gather.4.cloned.1.call-start = ((), (), s32[]{:S(2)}) async-start(), calls=%async_computation.2 | async-start | bytes 2359296 | tf_op jit(solution)/shard_map/all_gather | solution.py:205
  12.2 110.9 %all-gather.6.cloned.1.call-start = ((), (), s32[]{:S(2)}) async-start(), calls=%async_computation.4 | async-start | bytes 4456448 | tf_op jit(solution)/shard_map/all_gather | solution.py:207
  12.2 1.6 collective-permute-start
  13.8 0.7 copy-start.6
  14.6 173.0 %reduce-scatter.2.cloned.1.call-start = ((), (), s32[]{:S(2)}) async-start(), calls=%async_computation.3 | async-start | bytes 4718592 | tf_op jit(solution)/shard_map/reduce_scatter | solution.py:215
  14.6 65.7 %collective-permute-start.3 = (bf16[512,512]{1,0:T(8,128)(2,1)S(1)}, bf16[512,512]{1,0:T(8,128)(2,1)S(1)}, u32[]{:S(2)}, u32[]{:S(2)}) collective-permute-start(bf16[512,512]{1,0:T(8,128)(2,1)S(1)} %copy-done), channel_id=1, source_target_pairs={{0,128},{128,0},{1,129},{129,1},{2,130},{130,2},{3,131},{131,3},{4... | collective-permute-start | bytes 1572872 | tf_op jit(solution)/shard_map/ppermute | solution.py:198
  16.8 106.3 %collective-permute-start.1 = (bf16[512,512]{1,0:T(8,128)(2,1)S(1)}, bf16[512,512]{1,0:T(8,128)(2,1)S(1)}, u32[]{:S(2)}, u32[]{:S(2)}) collective-permute-start(bf16[512,512]{1,0:T(8,128)(2,1)S(1)} %copy-done.1), channel_id=1, source_target_pairs={{0,128},{128,0},{1,129},{129,1},{2,130},{130,2},{3,131},{131,3},{4... | collective-permute-start | bytes 1572872 | tf_op jit(solution)/shard_map/ppermute | solution.py:199
  18.2 104.8 %collective-permute-start.2 = (bf16[512,512]{1,0:T(8,128)(2,1)S(1)}, bf16[512,512]{1,0:T(8,128)(2,1)S(1)}, u32[]{:S(2)}, u32[]{:S(2)}) collective-permute-start(bf16[512,512]{1,0:T(8,128)(2,1)S(1)} %copy-done.2), channel_id=1, source_target_pairs={{0,128},{128,0},{1,129},{129,1},{2,130},{130,2},{3,131},{131,3},{4... | collective-permute-start | bytes 1572872 | tf_op jit(solution)/shard_map/ppermute | solution.py:200
  80.3 0.8 copy-start.5
  123.1 0.8 copy-start.3
  123.1 1.0 copy-start.4
Sparse Core Ops, SparseCore 0:
  12.3 50.6 all-gather.3
  64.8 42.8 all-gather.5
  135.8 51.7 reduce-scatter.1
